TPU v7x, 32 devices: a whole 2x2x4 slice. The times are simulated.
32 devices in a mesh: dp: 8 (over y, x, core), tensor: 4 (over z).
Axes of the slice: x: 2, y: 2, z: 4, core: 2. Of those that a mesh axis runs over, the one named last changes fastest.
Arguments:
- x_in: bfloat16 [16384, 768], P(('dp', 'tensor')), may hold values from -6 to 6
- bucket: int32 [32], P(('dp', 'tensor')), may hold values from 0 to 1
- lengths: int32 [32, 4], P(('dp', 'tensor')), may hold values from 32 to 128, as said below
- qkv_weight: bfloat16 [2, 768, 2304], replicated, may hold values from -0.21875 to 0.21875
- out_weight: bfloat16 [2, 768, 768], replicated, may hold values from -0.875 to 0.875
- norm_gain1: float32 [2, 768], replicated, may hold values from 0.5 to 1.5
- norm_bias1: float32 [2, 768], replicated, may hold values from -1.8 to 1.8
- up_weight: bfloat16 [2, 768, 2, 3072], P(None, None, None, 'tensor'), may hold values from -0.21875 to 0.21875
- down_weight: bfloat16 [2, 3072, 768], P(None, 'tensor'), may hold values from -0.109375 to 0.109375
- norm_gain2: float32 [2, 768], replicated, may hold values from 0.5 to 1.5
- norm_bias2: float32 [2, 768], replicated, may hold values from -1.8 to 1.8
- cotangent: bfloat16 [16384, 768], P(('dp', 'tensor')), may hold values from -6 to 6
Outputs:
- activations: bfloat16 [2, 16384, 768], P(None, ('dp', 'tensor'))
- input_grad: float32 [16384, 768], P(('dp', 'tensor'))
- qkv_grad: float32 [2, 768, 2304], replicated
- out_grad: float32 [2, 768, 768], replicated
- gain1_grad: float32 [2, 768], replicated
- bias1_grad: float32 [2, 768], replicated
- up_grad: float32 [2, 768, 2, 3072], P(None, 'dp', None, 'tensor')
- down_grad: float32 [2, 3072, 768], P(None, 'tensor', 'dp')
- gain2_grad: float32 [2, 768], replicated
- bias2_grad: float32 [2, 768], replicated
Inputs may be any that keep to these rules, and one draw needn't show every extreme that they name: Every entry is a length of a short sequence; each row of lengths has an entry equal to 128. A block of bucket 1 holds one sequence whose length is the sum of its row of lengths.
All inputs are finite; a program needn't handle non-finite values.
Results may differ from a plain program's by a relative error of at most 0.033.
Values may be sent and summed in bfloat16 or wider, within the bound.
No kernel may reach another device: no remote copies, remote signals or barrier semaphores. Data moves between devices by JAX's collectives and lax.ppermute only.
A program may use at most 256 MiB of HBM per device.

v0:
```python
import jax
import jax.numpy as jnp
from jax import lax
from jax.sharding import PartitionSpec as P

HEADS = 12
HEAD_DIM = 64
SHORT = 128
LAYERS = 2
eps_norm = 1e-05
gelu_coef = 0.7978845608028654
masked_score = -1e30


def segments(bucket_one, lens, rows_dev, short_len):
    rows = jnp.arange(rows_dev, dtype=jnp.int32)
    slot = rows // short_len
    offset = rows - slot * short_len
    slots_all = jnp.arange(lens.shape[0], dtype=jnp.int32)
    slot_len = jnp.sum(jnp.where(slot[:, None] == slots_all[None, :], lens[None, :], 0), axis=1)
    total = jnp.sum(lens)
    is_long = bucket_one == 1
    real = jnp.where(is_long, rows < total, offset < slot_len)
    group = jnp.where(is_long, 0, slot)
    return jnp.where(real, group, lens.shape[0] + rows)


def alibi(rows_dev, heads):
    slopes = jnp.exp2(-8.0 * (jnp.arange(heads, dtype=jnp.float32) + 1.0) / heads)
    place = jnp.arange(rows_dev, dtype=jnp.float32)
    dist = jnp.abs(place[:, None] - place[None, :])
    return slopes[:, None, None] * dist[None, :, :]


def layer_norm(value, gain, bias):
    mean = jnp.mean(value, axis=-1, keepdims=True)
    centered = value - mean
    var = jnp.mean(centered * centered, axis=-1, keepdims=True)
    return centered * lax.rsqrt(var + eps_norm) * gain + bias


def geglu(joined):
    half = joined.shape[1] // 2
    gate = joined[:, :half]
    value = joined[:, half:]
    return 0.5 * gate * (1.0 + jnp.tanh(gelu_coef * (gate + 0.044715 * gate * gate * gate))) * value


def split_heads(qkv_low, width):
    rows = qkv_low.shape[0]
    query = qkv_low[:, :width].reshape(rows, HEADS, HEAD_DIM)
    keys = qkv_low[:, width : 2 * width].reshape(rows, HEADS, HEAD_DIM)
    values = qkv_low[:, 2 * width :].reshape(rows, HEADS, HEAD_DIM)
    return (query, keys, values)


def scores_of(query, keys, same, decay):
    raw = (
        jnp.einsum("qhe,khe->hqk", query, keys, preferred_element_type=jnp.float32)
        * HEAD_DIM ** (-0.5)
        - decay
    )
    return jnp.where(same[None, :, :], raw, masked_score)


def forward_layer(x_low, wqkv, wo, g1, b1, wup, wdown, g2, b2, same, decay):
    rows = x_low.shape[0]
    width = x_low.shape[1]
    qkv_low = jnp.dot(x_low, wqkv, preferred_element_type=jnp.float32).astype(jnp.bfloat16)
    query, keys, values = split_heads(qkv_low, width)
    scores = scores_of(query, keys, same, decay)
    top = jnp.max(scores, axis=-1, keepdims=True)
    log_total = top + jnp.log(jnp.sum(jnp.exp(scores - top), axis=-1, keepdims=True))
    probs_low = jnp.exp(scores - log_total).astype(jnp.bfloat16)
    ctx_low = (
        jnp.einsum("hqk,khe->qhe", probs_low, values, preferred_element_type=jnp.float32)
        .reshape(rows, width)
        .astype(jnp.bfloat16)
    )
    attn = jnp.dot(ctx_low, wo, preferred_element_type=jnp.float32)
    pre_first = x_low.astype(jnp.float32) + attn
    normed = layer_norm(pre_first, g1, b1)
    normed_low = normed.astype(jnp.bfloat16)
    gathered = lax.all_gather(normed_low, "tensor", axis=0, tiled=True)
    joined = jnp.dot(gathered, wup.reshape(width, -1), preferred_element_type=jnp.float32)
    act_low = geglu(joined).astype(jnp.bfloat16)
    mixed = lax.psum_scatter(
        jnp.dot(act_low, wdown, preferred_element_type=jnp.float32).astype(jnp.bfloat16),
        "tensor",
        scatter_dimension=0,
        tiled=True,
    ).astype(jnp.float32)
    pre_second = normed + mixed
    out_low = layer_norm(pre_second, g2, b2).astype(jnp.bfloat16)
    keep = (
        x_low,
        qkv_low,
        log_total,
        ctx_low,
        pre_first,
        normed_low,
        pre_second,
        gathered,
        joined,
        act_low,
    )
    return (out_low, keep)


def backward_layer(grad_out, keep, wqkv, wo, g1, b1, wup, wdown, g2, b2, same, decay):
    (
        x_low,
        qkv_low,
        log_total,
        ctx_low,
        pre_first,
        normed_low,
        pre_second,
        gathered,
        joined,
        act_low,
    ) = keep
    rows = x_low.shape[0]
    width = x_low.shape[1]
    up_flat = wup.reshape(width, -1)
    second_pull = jax.vjp(layer_norm, pre_second, g2, b2)[1]
    d_pre2, d_gain2, d_bias2 = second_pull(grad_out)
    grad_rows = lax.all_gather(d_pre2.astype(jnp.bfloat16), "tensor", axis=0, tiled=True)
    d_act = jnp.dot(grad_rows, wdown.T, preferred_element_type=jnp.float32)
    d_down = jnp.dot(act_low.T, grad_rows, preferred_element_type=jnp.float32)
    geglu_pull = jax.vjp(geglu, joined)[1]
    d_joined = geglu_pull(d_act)[0].astype(jnp.bfloat16)
    d_up = jnp.dot(gathered.T, d_joined, preferred_element_type=jnp.float32).reshape(wup.shape)
    d_normed = d_pre2 + lax.psum_scatter(
        jnp.dot(d_joined, up_flat.T, preferred_element_type=jnp.float32).astype(jnp.bfloat16),
        "tensor",
        scatter_dimension=0,
        tiled=True,
    ).astype(jnp.float32)
    first_pull = jax.vjp(layer_norm, pre_first, g1, b1)[1]
    d_pre1, d_gain1, d_bias1 = first_pull(d_normed)
    d_attn_low = d_pre1.astype(jnp.bfloat16)
    d_wo = jnp.dot(ctx_low.T, d_attn_low, preferred_element_type=jnp.float32)
    d_ctx = (
        jnp.dot(d_attn_low, wo.T, preferred_element_type=jnp.float32)
        .astype(jnp.bfloat16)
        .reshape(rows, HEADS, HEAD_DIM)
    )
    query, keys, values = split_heads(qkv_low, width)
    probs = jnp.exp(scores_of(query, keys, same, decay) - log_total)
    probs_low = probs.astype(jnp.bfloat16)
    d_values = jnp.einsum("hqk,qhe->khe", probs_low, d_ctx, preferred_element_type=jnp.float32)
    d_probs = jnp.einsum("qhe,khe->hqk", d_ctx, values, preferred_element_type=jnp.float32)
    d_scores = (probs * (d_probs - jnp.sum(probs * d_probs, axis=-1, keepdims=True))).astype(
        jnp.bfloat16
    )
    d_query = jnp.einsum(
        "hqk,khe->qhe", d_scores, keys, preferred_element_type=jnp.float32
    ) * HEAD_DIM ** (-0.5)
    d_keys = jnp.einsum(
        "hqk,qhe->khe", d_scores, query, preferred_element_type=jnp.float32
    ) * HEAD_DIM ** (-0.5)
    d_qkv = jnp.concatenate(
        [d_query.reshape(rows, width), d_keys.reshape(rows, width), d_values.reshape(rows, width)],
        axis=1,
    ).astype(jnp.bfloat16)
    d_wqkv = jnp.dot(x_low.T, d_qkv, preferred_element_type=jnp.float32)
    d_input = d_pre1 + jnp.dot(d_qkv, wqkv.T, preferred_element_type=jnp.float32)
    return (d_input, d_wqkv, d_wo, d_gain1, d_bias1, d_up, d_down, d_gain2, d_bias2)


def shards(
    x_in,
    bucket,
    lengths,
    qkv_weight,
    out_weight,
    norm_gain1,
    norm_bias1,
    up_weight,
    down_weight,
    norm_gain2,
    norm_bias2,
    cotangent,
):
    rows = x_in.shape[0]
    seg = segments(bucket[0], lengths[0], rows, SHORT)
    same = seg[:, None] == seg[None, :]
    decay = alibi(rows, HEADS)
    layer_in = x_in
    outputs = []
    kept = []
    for layer in range(LAYERS):
        layer_in, keep = forward_layer(
            layer_in,
            qkv_weight[layer],
            out_weight[layer],
            norm_gain1[layer],
            norm_bias1[layer],
            up_weight[layer],
            down_weight[layer],
            norm_gain2[layer],
            norm_bias2[layer],
            same,
            decay,
        )
        outputs.append(layer_in)
        kept.append(keep)
    grad = cotangent.astype(jnp.float32)
    found = [None] * LAYERS
    for layer in reversed(range(LAYERS)):
        grad, d_wqkv, d_wo, d_gain1, d_bias1, d_up, d_down, d_gain2, d_bias2 = backward_layer(
            grad,
            kept[layer],
            qkv_weight[layer],
            out_weight[layer],
            norm_gain1[layer],
            norm_bias1[layer],
            up_weight[layer],
            down_weight[layer],
            norm_gain2[layer],
            norm_bias2[layer],
            same,
            decay,
        )
        d_wqkv, d_wo, d_gain1, d_bias1, d_gain2, d_bias2 = lax.psum(
            (d_wqkv, d_wo, d_gain1, d_bias1, d_gain2, d_bias2), ("dp", "tensor")
        )
        d_up, d_down = (
            lax.psum_scatter(
                d_up.astype(jnp.bfloat16), "dp", scatter_dimension=0, tiled=True
            ).astype(jnp.float32),
            lax.psum_scatter(
                d_down.astype(jnp.bfloat16), "dp", scatter_dimension=1, tiled=True
            ).astype(jnp.float32),
        )
        found[layer] = (d_wqkv, d_wo, d_gain1, d_bias1, d_up, d_down, d_gain2, d_bias2)
    stacked = [jnp.stack([found[layer][index] for layer in range(LAYERS)]) for index in range(8)]
    qkv_grad, out_grad, gain1_grad, bias1_grad, up_grad, down_grad, gain2_grad, bias2_grad = stacked
    activations = jnp.stack(outputs)
    return (
        activations,
        grad,
        qkv_grad,
        out_grad,
        gain1_grad,
        bias1_grad,
        up_grad,
        down_grad,
        gain2_grad,
        bias2_grad,
    )


def solution(mesh):
    in_specs = (
        P(("dp", "tensor"), None),
        P(("dp", "tensor")),
        P(("dp", "tensor"), None),
        P(),
        P(),
        P(),
        P(),
        P(None, None, None, "tensor"),
        P(None, "tensor", None),
        P(),
        P(),
        P(("dp", "tensor"), None),
    )
    out_specs = (
        P(None, ("dp", "tensor"), None),
        P(("dp", "tensor"), None),
        P(),
        P(),
        P(),
        P(),
        P(None, "dp", None, "tensor"),
        P(None, "tensor", "dp"),
        P(),
        P(),
    )
    return jax.shard_map(shards, mesh=mesh, in_specs=in_specs, out_specs=out_specs, check_vma=False)
```

profile of v0, /device:TPU:0, one launch (start us, length us, event | category | flops | bytes accessed | tf_op | source)
XLA Modules:
  0.0 1206.9 jit_solution(10613801410674038543)
XLA Ops:
  32.5 7.0 fusion.100
  41.4 57.2 %all-gather.5.cloned.1.call-done = bf16[2048,768]{1,0:T(8,128)(2,1)} async-done(((bf16[512,768]{1,0:T(8,128)(2,1)}), bf16[2048,768]{1,0:T(8,128)(2,1)}) %all-gather.5.cloned.1.call-update) | async-done | bytes 3145744 | tf_op jit(solution)/shard_map/all_gather | solution.py:84
  98.6 7.7 fusion.107
  117.8 58.3 %reduce-scatter.7.cloned.1.call-done = bf16[512,768]{1,0:T(8,128)(2,1)} async-done(((bf16[2048,768]{1,0:T(8,128)(2,1)}), bf16[512,768]{1,0:T(8,128)(2,1)}) %reduce-scatter.7.cloned.1.call-update) | async-done | bytes 786448 | tf_op jit(solution)/shard_map/reduce_scatter | solution.py:87
  205.4 60.0 %all-gather.7.cloned.1.call-done = bf16[2048,768]{1,0:T(8,128)(2,1)} async-done(((bf16[512,768]{1,0:T(8,128)(2,1)}), bf16[2048,768]{1,0:T(8,128)(2,1)}) %all-gather.7.cloned.1.call-update) | async-done | bytes 3145744 | tf_op jit(solution)/shard_map/all_gather | solution.py:84
  265.3 7.7 fusion.108
  283.7 59.0 %reduce-scatter.9.cloned.1.call-done = bf16[512,768]{1,0:T(8,128)(2,1)} async-done(((bf16[2048,768]{1,0:T(8,128)(2,1)}), bf16[512,768]{1,0:T(8,128)(2,1)}) %reduce-scatter.9.cloned.1.call-update) | async-done | bytes 786448 | tf_op jit(solution)/shard_map/reduce_scatter | solution.py:87
  350.1 63.4 %all-gather.9.cloned.1.call-done = bf16[2048,768]{1,0:T(8,128)(2,1)} async-done(((bf16[512,768]{1,0:T(8,128)(2,1)}), bf16[2048,768]{1,0:T(8,128)(2,1)}) %all-gather.9.cloned.1.call-update) | async-done | bytes 3145744 | tf_op jit(solution)/shard_map/all_gather | solution.py:128
  413.6 12.0 fusion.25
  436.7 59.0 %reduce-scatter.11.cloned.1.call-done = bf16[512,768]{1,0:T(8,128)(2,1)} async-done(((bf16[2048,768]{1,0:T(8,128)(2,1)}), bf16[512,768]{1,0:T(8,128)(2,1)}) %reduce-scatter.11.cloned.1.call-update) | async-done | bytes 786448 | tf_op jit(solution)/shard_map/reduce_scatter | solution.py:134
  502.1 7.7 fusion.51
  509.8 9.2 multiply_reduce_fusion.1
  536.6 63.6 %all-gather.11.cloned.1.call-done = bf16[2048,768]{1,0:T(8,128)(2,1)} async-done(((bf16[512,768]{1,0:T(8,128)(2,1)}), bf16[2048,768]{1,0:T(8,128)(2,1)}) %all-gather.11.cloned.1.call-update) | async-done | bytes 3145744 | tf_op jit(solution)/shard_map/all_gather | solution.py:128
  600.3 12.6 %fusion.24 = (f32[2048,768]{1,0:T(8,128)S(1)}, f32[2048,768]{1,0:T(8,128)S(1)}) fusion(f32[2048,1536]{1,0:T(8,128)} %copy-done.8, bf16[2048,768]{1,0:T(8,128)(2,1)} %all-gather.11.cloned.1.call-done, bf16[2,768,768]{2,1,0:T(8,128)(2,1)} %param.20), kind=kOutput, calls=%fused_computation.69 | convolution fusion | flops 2456813568 | bytes 29491200 | tf_op jit(solution)/shard_map/dot_general | solution.py:129
  630.9 12.0 convolution_convert_fusion.2
  664.5 9.3 convolution_convert_fusion.3
  691.0 10.9 multiply_reduce_fusion
  704.0 7.0 multiply_convert_fusion
  728.1 35.8 %reduce-scatter.15.cloned.1.call-done = bf16[768,96]{0,1:T(8,128)(2,1)} async-done(((bf16[768,768]{0,1:T(8,128)(2,1)}), bf16[768,96]{0,1:T(8,128)(2,1)}) %reduce-scatter.15.cloned.1.call-update) | async-done | bytes 147472 | tf_op jit(solution)/shard_map/reduce_scatter | solution.py:233
  765.8 88.5 %all-reduce.14.cloned.1.call-done = (bf16[768,2,768]{2,1,0:T(2,128)(2,1)}, bf16[768,2,768]{2,1,0:T(2,128)(2,1)}) async-done(((bf16[768,2,768]{2,1,0:T(2,128)(2,1)}, bf16[768,2,768]{2,1,0:T(2,128)(2,1)}), (bf16[768,2,768]{2,1,0:T(2,128)(2,1)}, bf16[768,2,768]{2,1,0:T(2,128)(2,1)})) %all-reduce.14.cloned.1.call-update) | async-done | bytes 4718608
  858.5 41.8 %all-reduce.6 = (f32[1,768]{1,0:T(1,128)S(1)}, f32[1,768]{1,0:T(1,128)S(1)}, f32[1,768]{1,0:T(1,128)S(1)}, f32[1,768]{1,0:T(1,128)S(1)}, f32[1,768]{1,0:T(1,128)...) all-reduce(f32[1,768]{1,0:T(1,128)S(1)} %stack.101, ...), channel_id=1, replica_groups=mesh['dp'=8,'tensor'=4] {'dp','tensor'}, use_global_device_ids=true, to_apply=%region_35.36 | all-reduce | flops 6144 | bytes 49152 | tf_op jit(solution)/shard_map/psum | solution.py:226
  908.2 260.8 %all-reduce.12.cloned.1.call-done = (f32[1,768,2304]{1,2,0:T(8,128)}, f32[1,768,2304]{1,2,0:T(8,128)}, f32[1,768,768]{2,1,0:T(8,128)}, f32[1,768,768]{2,1,0:T(8,128)}) async-done(((f32[1,768,2304]{1,2,0:T(8,128)}, f32[1,768,2304]{1,2,0:T(8,128)}, f32[1,768,768]{2,1,0:T(8,128)}, f32[1,768,768]{2,1,0:T(8,128)}), (f32[1,768,2304]{1,2,0:T(8,128)}, f32[1,768,2304]{1,2,0:T(8,128)}, f32[1,768,768]{2,1,0:T(8,128)}, ...) | async-done | bytes 18874384 | tf_op jit(solution)/shard_map/psum | solution.py:226
  1169.0 11.0 pad_maximum_fusion
  1179.9 15.4 %copy.101 = f32[2,768,2304]{2,1,0:T(8,128)} copy(f32[2,768,2304]{1,2,0:T(8,128)} %pad_maximum_fusion) | data formatting | bytes 28311552
  (326 shorter events, 212.5 us)
Async XLA Ops:
  7.2 91.5 %all-gather.5.cloned.1.call-start = ((), (), s32[]{:S(2)}) async-start(), calls=%async_computation.6 | async-start | bytes 3932160 | tf_op jit(solution)/shard_map/all_gather | solution.py:84
  29.9 146.2 %copy-start.2 = (f32[512,768]{1,0:T(8,128)}, f32[512,768]{1,0:T(8,128)S(1)}, u32[]{:S(2)}) copy-start(f32[512,768]{1,0:T(8,128)S(1)} %get-tuple-element.112) | copy-start | bytes 4718596
  30.0 146.2 %copy-start.53 = (f32[512]{0:T(512)}, f32[512]{0:T(512)S(1)}, u32[]{:S(2)}) copy-start(f32[512]{0:T(512)S(1)} %broadcast_multiply_fusion.3) | copy-start | bytes 6148
  31.0 145.1 %copy-start.55 = (f32[512]{0:T(512)}, f32[512]{0:T(512)S(1)}, u32[]{:S(2)}) copy-start(f32[512]{0:T(512)S(1)} %fusion.80) | copy-start | bytes 6148
  31.1 145.1 %copy-start.51 = (f32[768]{0:T(1024)}, f32[768]{0:T(1024)S(1)}, u32[]{:S(2)}) copy-start(f32[768]{0:T(1024)S(1)} %get-tuple-element.122) | copy-start | bytes 9220
  32.3 143.8 %reduce-scatter.7.cloned.1.call-start = ((), (), s32[]{:S(2)}) async-start(), calls=%async_computation.7 | async-start | bytes 3932160 | tf_op jit(solution)/shard_map/reduce_scatter | solution.py:87
  117.0 148.3 %all-gather.7.cloned.1.call-start = ((), (), s32[]{:S(2)}) async-start(), calls=%async_computation.8 | async-start | bytes 3932160 | tf_op jit(solution)/shard_map/all_gather | solution.py:84
  117.8 81.4 %copy-start.59 = (f32[768]{0:T(1024)}, f32[768]{0:T(1024)S(1)}, u32[]{:S(2)}) copy-start(f32[768]{0:T(1024)S(1)} %get-tuple-element.65) | copy-start | bytes 9220
  201.7 141.1 %reduce-scatter.9.cloned.1.call-start = ((), (), s32[]{:S(2)}) async-start(), calls=%async_computation.9 | async-start | bytes 3932160 | tf_op jit(solution)/shard_map/reduce_scatter | solution.py:87
  283.7 129.9 %all-gather.9.cloned.1.call-start = ((), (), s32[]{:S(2)}) async-start(), calls=%async_computation.10 | async-start | bytes 3932160 | tf_op jit(solution)/shard_map/all_gather | solution.py:128
  349.9 145.8 %reduce-scatter.11.cloned.1.call-start = ((), (), s32[]{:S(2)}) async-start(), calls=%async_computation.11 | async-start | bytes 3932160 | tf_op jit(solution)/shard_map/reduce_scatter | solution.py:134
  413.6 16.6 %copy-start.40 = (bf16[96,8,2,768]{3,1,2,0:T(8,128)(2,1)S(1)}, bf16[96,8,2,768]{3,1,2,0:T(8,128)(2,1)}, u32[]{:S(2)}) copy-start(bf16[96,8,2,768]{3,1,2,0:T(8,128)(2,1)} %copy.112) | copy-start | bytes 7077892
  436.6 163.6 %all-gather.11.cloned.1.call-start = ((), (), s32[]{:S(2)}) async-start(), calls=%async_computation.12 | async-start | bytes 3932160 | tf_op jit(solution)/shard_map/all_gather | solution.py:128
  502.1 16.9 %slice-start.3 = ((s8[12582912]{0:T(1024)(128)(4,1)}), s8[4194304]{0:T(1024)(128)(4,1)S(1)}, s32[]{:S(2)}) async-start(s8[12582912]{0:T(1024)(128)(4,1)} %bitcast.151), calls=%async_computation.21 | async-start | bytes 8388608
  502.1 16.9 %slice-start.4 = ((s8[12582912]{0:T(1024)(128)(4,1)}), s8[4194304]{0:T(1024)(128)(4,1)S(1)}, s32[]{:S(2)}) async-start(s8[12582912]{0:T(1024)(128)(4,1)} %bitcast.151), calls=%async_computation.22 | async-start | bytes 8388608
  536.6 146.5 %reduce-scatter.13.cloned.1.call-start = ((), (), s32[]{:S(2)}) async-start(), calls=%async_computation.13 | async-start | bytes 3932160 | tf_op jit(solution)/shard_map/reduce_scatter | solution.py:134
  600.3 17.3 %copy-start.39 = (bf16[96,8,2,768]{3,1,2,0:T(8,128)(2,1)S(1)}, bf16[96,8,2,768]{3,1,2,0:T(8,128)(2,1)}, u32[]{:S(2)}) copy-start(bf16[96,8,2,768]{3,1,2,0:T(8,128)(2,1)} %copy.111) | copy-start | bytes 7077892
  624.0 104.1 %reduce-scatter.17.cloned.1.call-start = ((), (), s32[]{:S(2)}) async-start(), calls=%async_computation.15 | async-start | bytes 1327104 | tf_op jit(solution)/shard_map/reduce_scatter | solution.py:233
  630.6 133.3 %reduce-scatter.15.cloned.1.call-start = ((), (), s32[]{:S(2)}) async-start(), calls=%async_computation.14 | async-start | bytes 1327104 | tf_op jit(solution)/shard_map/reduce_scatter | solution.py:233
  655.5 198.8 %all-reduce.14.cloned.1.call-start = ((), (), s32[]{:S(2)}) async-start(), calls=%async_computation.17 | async-start | bytes 9437184
  679.8 489.2 %all-reduce.12.cloned.1.call-start = ((), (), s32[]{:S(2)}) async-start(), calls=%async_computation.16 | async-start | bytes 37748736 | tf_op jit(solution)/shard_map/psum | solution.py:226
  728.0 174.6 %copy-start.20 = (f32[512,768]{1,0:T(8,128)S(1)}, f32[512,768]{1,0:T(8,128)}, u32[]{:S(2)}) copy-start(f32[512,768]{1,0:T(8,128)} %copy-done.18) | copy-start | bytes 4718596
  728.0 174.6 %copy-start.36 = (bf16[12,64,512]{2,1,0:T(8,128)(2,1)S(1)}, bf16[12,64,512]{2,1,0:T(8,128)(2,1)}, u32[]{:S(2)}) copy-start(bf16[12,64,512]{2,1,0:T(8,128)(2,1)} %copy-done.35) | copy-start | bytes 2359300
  728.0 174.6 %copy-start.45 = (bf16[12,64,512]{2,1,0:T(8,128)(2,1)S(1)}, bf16[12,64,512]{2,1,0:T(8,128)(2,1)}, u32[]{:S(2)}) copy-start(bf16[12,64,512]{2,1,0:T(8,128)(2,1)} %copy-done.44) | copy-start | bytes 2359300
  (81 other events, 314.6 us)
Sparse Core Ops, SparseCore 0:
  32.4 66.1 all-gather.4
  117.2 58.8 reduce-scatter.6
  201.8 63.5 all-gather.6
  283.8 58.8 reduce-scatter.8
  350.0 63.5 all-gather.8
  436.7 58.8 reduce-scatter.10
  536.7 63.5 all-gather.10
  624.2 58.8 reduce-scatter.12
  686.9 36.8 reduce-scatter.16
  727.2 36.7 reduce-scatter.14
  767.3 86.9 all-reduce.13
  862.3 306.5 all-reduce.11
where the time goes:
time: 1220 us; the launch traced here: 1210 us
  waiting for transfers between devices  809 us (66%)
  matrix products  182 us (15%)
  local copies, waits for them, and re-layouts  85.4 us (7%)
  other arithmetic  69 us (6%)
  blocking collectives  41.8 us (3%)
  between operations  17.3 us (1%)
    psum x1, waiting for transfers between devices, shards(): lax.psum((d_wqkv, d_wo, d_gain1, d_bias1, d_gain2, d_bias2), ('dp', 'tens...  261 us
    all_gather x2, waiting for transfers between devices, backward_layer(): lax.all_gather(d_pre2.astype(jnp.bfloat16), 'tensor', axis=0, tiled=True)  127 us
    reduce_scatter x2, waiting for transfers between devices, forward_layer(): lax.psum_scatter(jnp.dot(act_low, wdown, preferred_element_type=jnp.float...  117 us
    all_gather x2, waiting for transfers between devices, forward_layer(): gathered = lax.all_gather(normed_low, 'tensor', axis=0, tiled=True)  117 us
    unnamed x13, waiting for transfers between devices  88.7 us
    reduce_scatter x2, waiting for transfers between devices, backward_layer(): lax.psum_scatter(jnp.dot(d_joined, up_flat.T, preferred_element_type=jnp....  62.3 us
    unnamed x190, local copies, waits for them, and re-layouts  56 us
    psum x1, blocking collectives, shards(): lax.psum((d_wqkv, d_wo, d_gain1, d_bias1, d_gain2, d_bias2), ('dp', 'tens...  41.8 us
  transfers between devices with their start and end apart: 12, of which 11 were waited for; matrix products, arithmetic and copies ran while one was open for 10% of the time, Pallas kernels for 0%

commit v1 on v0

--- a/solution.py
+++ b/solution.py
@@ -10,6 +10,18 @@
 eps_norm = 1e-05
 gelu_coef = 0.7978845608028654
 masked_score = -1e30
+
+
+def gather_by_bits(array, axis, dim):
+    ways, here = (lax.axis_size(axis), lax.axis_index(axis))
+    grown, reach = (array, 1)
+    while reach < ways:
+        theirs = lax.ppermute(grown, axis, [(d, d ^ reach) for d in range(ways)])
+        mine_first = jnp.concatenate([grown, theirs], axis=dim)
+        theirs_first = jnp.concatenate([theirs, grown], axis=dim)
+        grown = jnp.where(here & reach == 0, mine_first, theirs_first)
+        reach = 2 * reach
+    return grown
 
 
 def segments(bucket_one, lens, rows_dev, short_len):
@@ -125,7 +137,7 @@
     up_flat = wup.reshape(width, -1)
     second_pull = jax.vjp(layer_norm, pre_second, g2, b2)[1]
     d_pre2, d_gain2, d_bias2 = second_pull(grad_out)
-    grad_rows = lax.all_gather(d_pre2.astype(jnp.bfloat16), "tensor", axis=0, tiled=True)
+    grad_rows = gather_by_bits(d_pre2.astype(jnp.bfloat16), "tensor", 0)
     d_act = jnp.dot(grad_rows, wdown.T, preferred_element_type=jnp.float32)
     d_down = jnp.dot(act_low.T, grad_rows, preferred_element_type=jnp.float32)
     geglu_pull = jax.vjp(geglu, joined)[1]

time: 1220 us -> 1280 us (1.049)
  waiting for transfers between devices: 809 us -> 853 us
    ppermute x0 -> x4, waiting for transfers between devices: none -> 171 us  [gather_by_bits(): theirs = lax.ppermute(grown, axis, [(d, d ^ reach) for d in range(ways)])]
    all_gather x2 -> x0, waiting for transfers between devices: 127 us -> none  [backward_layer(): lax.all_gather(d_pre2.astype(jnp.bfloat16), 'tensor', axis=0, tiled=True)]
    unnamed x190 -> x188, local copies, waits for them, and re-layouts: 56 us -> 49.6 us
    unnamed x13 -> x11, waiting for transfers between devices: 88.7 us -> 88.7 us
  transfers between devices with their start and end apart: 12 -> 14, of which waited for: 11 -> 13; matrix products, arithmetic and copies ran while one was open for 10% -> 10% of each run, Pallas kernels for 0% -> 0%
where the time goes in v1:
time: 1280 us; the launch traced here: 1270 us
  waiting for transfers between devices  853 us (67%)
  matrix products  194 us (15%)
  local copies, waits for them, and re-layouts  79.3 us (6%)
  other arithmetic  73.6 us (6%)
  blocking collectives  41.8 us (3%)
  between operations  16.9 us (1%)
    psum x1, waiting for transfers between devices, shards(): lax.psum((d_wqkv, d_wo, d_gain1, d_bias1, d_gain2, d_bias2), ('dp', 'tens...  261 us
    ppermute x4, waiting for transfers between devices, gather_by_bits(): theirs = lax.ppermute(grown, axis, [(d, d ^ reach) for d in range(ways)])  171 us
    reduce_scatter x2, waiting for transfers between devices, forward_layer(): lax.psum_scatter(jnp.dot(act_low, wdown, preferred_element_type=jnp.float...  117 us
    all_gather x2, waiting for transfers between devices, forward_layer(): gathered = lax.all_gather(normed_low, 'tensor', axis=0, tiled=True)  117 us
    unnamed x11, waiting for transfers between devices  88.7 us
    reduce_scatter x2, waiting for transfers between devices, backward_layer(): lax.psum_scatter(jnp.dot(d_joined, up_flat.T, preferred_element_type=jnp....  63 us
    unnamed x188, local copies, waits for them, and re-layouts  49.6 us
    psum x1, blocking collectives, shards(): lax.psum((d_wqkv, d_wo, d_gain1, d_bias1, d_gain2, d_bias2), ('dp', 'tens...  41.8 us
  transfers between devices with their start and end apart: 14, of which 13 were waited for; matrix products, arithmetic and copies ran while one was open for 10% of the time, Pallas kernels for 0%

profile of v1, /device:TPU:0, one launch (start us, length us, event | category | flops | bytes accessed | tf_op | source)
XLA Modules:
  0.0 1267.8 jit_solution(17815977652460607213)
XLA Ops:
  41.6 57.0 %all-gather.3.cloned.1.call-done = bf16[2048,768]{1,0:T(8,128)(2,1)} async-done(((bf16[512,768]{1,0:T(8,128)(2,1)}), bf16[2048,768]{1,0:T(8,128)(2,1)}) %all-gather.3.cloned.1.call-update) | async-done | bytes 3145744 | tf_op jit(solution)/shard_map/all_gather | solution.py:96
  117.7 58.3 %reduce-scatter.7.cloned.1.call-done = bf16[512,768]{1,0:T(8,128)(2,1)} async-done(((bf16[2048,768]{1,0:T(8,128)(2,1)}), bf16[512,768]{1,0:T(8,128)(2,1)}) %reduce-scatter.7.cloned.1.call-update) | async-done | bytes 786448 | tf_op jit(solution)/shard_map/reduce_scatter | solution.py:99
  205.4 59.9 %all-gather.5.cloned.1.call-done = bf16[2048,768]{1,0:T(8,128)(2,1)} async-done(((bf16[512,768]{1,0:T(8,128)(2,1)}), bf16[2048,768]{1,0:T(8,128)(2,1)}) %all-gather.5.cloned.1.call-update) | async-done | bytes 3145744 | tf_op jit(solution)/shard_map/all_gather | solution.py:96
  284.1 58.6 %reduce-scatter.9.cloned.1.call-done = bf16[512,768]{1,0:T(8,128)(2,1)} async-done(((bf16[2048,768]{1,0:T(8,128)(2,1)}), bf16[512,768]{1,0:T(8,128)(2,1)}) %reduce-scatter.9.cloned.1.call-update) | async-done | bytes 786448 | tf_op jit(solution)/shard_map/reduce_scatter | solution.py:99
  350.8 18.4 %collective-permute-done = bf16[512,768]{1,0:T(8,128)(2,1)} collective-permute-done((bf16[512,768]{1,0:T(8,128)(2,1)}, bf16[512,768]{1,0:T(8,128)(2,1)}, u32[]{:S(2)}, u32[]{:S(2)}) %collective-permute-start) | collective-permute-done | bytes 786464 | tf_op jit(solution)/shard_map/ppermute | solution.py:19
  375.4 67.6 %collective-permute-done.1 = bf16[1024,768]{1,0:T(8,128)(2,1)} collective-permute-done((bf16[1024,768]{1,0:T(8,128)(2,1)}, bf16[1024,768]{1,0:T(8,128)(2,1)}, u32[]{:S(2)}, u32[]{:S(2)}) %collective-permute-start.1) | collective-permute-done | bytes 1572896 | tf_op jit(solution)/shard_map/ppermute | solution.py:19
  443.0 15.2 %fusion.25 = (f32[2048,768]{1,0:T(8,128)S(1)}, f32[2048,768]{1,0:T(8,128)}) fusion(f32[2048,1536]{1,0:T(8,128)} %copy-done.9, bf16[2,768,768]{2,1,0:T(8,128)(2,1)} %param.20, bf16[1024,768]{1,0:T(8,128)(2,1)} %collective-permute-done.1, bf16[1024,768]{1,0:T(8,128)(2,1)} %maximum_select_fusion.2, pred[]{:T(512)S(6)} %eq.52), kind=kOutput, calls=%fused_computation.72 | convolution fusion | flops 2470969344 | bytes 29491200 | tf_op jit(solution)/shard_map/dot_general | solution.py:141
  460.7 8.3 convolution_convert_fusion.7
  469.1 60.5 %reduce-scatter.11.cloned.1.call-done = bf16[512,768]{1,0:T(8,128)(2,1)} async-done(((bf16[2048,768]{1,0:T(8,128)(2,1)}), bf16[512,768]{1,0:T(8,128)(2,1)}) %reduce-scatter.11.cloned.1.call-update) | async-done | bytes 786448 | tf_op jit(solution)/shard_map/reduce_scatter | solution.py:146
  543.7 9.2 multiply_reduce_fusion.1
  570.6 18.1 %collective-permute-done.2 = bf16[512,768]{1,0:T(8,128)(2,1)S(1)} collective-permute-done((bf16[512,768]{1,0:T(8,128)(2,1)S(1)}, bf16[512,768]{1,0:T(8,128)(2,1)S(1)}, u32[]{:S(2)}, u32[]{:S(2)}) %collective-permute-start.2) | collective-permute-done | bytes 786464 | tf_op jit(solution)/shard_map/ppermute | solution.py:19
  592.2 67.3 %collective-permute-done.3 = bf16[1024,768]{1,0:T(8,128)(2,1)S(1)} collective-permute-done((bf16[1024,768]{1,0:T(8,128)(2,1)S(1)}, bf16[1024,768]{1,0:T(8,128)(2,1)S(1)}, u32[]{:S(2)}, u32[]{:S(2)}) %collective-permute-start.3) | collective-permute-done | bytes 1572896 | tf_op jit(solution)/shard_map/ppermute | solution.py:19
  659.5 14.6 %fusion.24 = (f32[2048,768]{1,0:T(8,128)}, f32[2048,768]{1,0:T(8,128)}) fusion(f32[2048,1536]{1,0:T(8,128)} %copy-done.8, bf16[2,768,768]{2,1,0:T(8,128)(2,1)S(1)} %copy-done.72, bf16[1024,768]{1,0:T(8,128)(2,1)S(1)} %collective-permute-done.3, bf16[1024,768]{1,0:T(8,128)(2,1)S(1)} %maximum_select_fusion.3, pred[]{:T(512)S(6)} %eq.52), kind=kOutput, calls=%fused_computation.71 | convolution fusion | flops 2470969344 | bytes 29491200 | tf_op jit(solution)/shard_map/dot_general | solution.py:141
  674.1 9.5 convolution_convert_fusion.6
  683.7 7.8 convolution_convert_fusion.8
  691.5 12.0 convolution_convert_fusion.2
  726.3 9.3 convolution_convert_fusion.3
  752.0 10.8 multiply_reduce_fusion
  790.4 34.8 %reduce-scatter.15.cloned.1.call-done = bf16[768,96]{0,1:T(8,128)(2,1)} async-done(((bf16[768,768]{0,1:T(8,128)(2,1)}), bf16[768,96]{0,1:T(8,128)(2,1)}) %reduce-scatter.15.cloned.1.call-update) | async-done | bytes 147472 | tf_op jit(solution)/shard_map/reduce_scatter | solution.py:245
  827.0 88.5 %all-reduce.14.cloned.1.call-done = (bf16[768,2,768]{2,1,0:T(2,128)(2,1)}, bf16[768,2,768]{2,1,0:T(2,128)(2,1)}) async-done(((bf16[768,2,768]{2,1,0:T(2,128)(2,1)}, bf16[768,2,768]{2,1,0:T(2,128)(2,1)}), (bf16[768,2,768]{2,1,0:T(2,128)(2,1)}, bf16[768,2,768]{2,1,0:T(2,128)(2,1)})) %all-reduce.14.cloned.1.call-update) | async-done | bytes 4718608
  919.7 41.8 %all-reduce.6 = (f32[1,768]{1,0:T(1,128)S(1)}, f32[1,768]{1,0:T(1,128)S(1)}, f32[1,768]{1,0:T(1,128)S(1)}, f32[1,768]{1,0:T(1,128)S(1)}, f32[1,768]{1,0:T(1,128)...) all-reduce(f32[1,768]{1,0:T(1,128)S(1)} %stack.101, ...), channel_id=1, replica_groups=mesh['dp'=8,'tensor'=4] {'dp','tensor'}, use_global_device_ids=true, to_apply=%region_35.36 | all-reduce | flops 6144 | bytes 49152 | tf_op jit(solution)/shard_map/psum | solution.py:238
  969.3 260.8 %all-reduce.12.cloned.1.call-done = (f32[1,768,2304]{1,2,0:T(8,128)}, f32[1,768,2304]{1,2,0:T(8,128)}, f32[1,768,768]{2,1,0:T(8,128)}, f32[1,768,768]{2,1,0:T(8,128)}) async-done(((f32[1,768,2304]{1,2,0:T(8,128)}, f32[1,768,2304]{1,2,0:T(8,128)}, f32[1,768,768]{2,1,0:T(8,128)}, f32[1,768,768]{2,1,0:T(8,128)}), (f32[1,768,2304]{1,2,0:T(8,128)}, f32[1,768,2304]{1,2,0:T(8,128)}, f32[1,768,768]{2,1,0:T(8,128)}, ...) | async-done | bytes 18874384 | tf_op jit(solution)/shard_map/psum | solution.py:238
  1230.2 11.0 pad_maximum_fusion
  1241.1 15.4 %copy.101 = f32[2,768,2304]{2,1,0:T(8,128)} copy(f32[2,768,2304]{1,2,0:T(8,128)} %pad_maximum_fusion) | data formatting | bytes 28311552
  (328 shorter events, 236.1 us)
Async XLA Ops:
  7.2 91.4 %all-gather.3.cloned.1.call-start = ((), (), s32[]{:S(2)}) async-start(), calls=%async_computation.6 | async-start | bytes 3932160 | tf_op jit(solution)/shard_map/all_gather | solution.py:96
  29.9 146.2 %copy-start.2 = (f32[512,768]{1,0:T(8,128)}, f32[512,768]{1,0:T(8,128)S(1)}, u32[]{:S(2)}) copy-start(f32[512,768]{1,0:T(8,128)S(1)} %get-tuple-element.112) | copy-start | bytes 4718596
  29.9 146.1 %copy-start.53 = (f32[512]{0:T(512)}, f32[512]{0:T(512)S(1)}, u32[]{:S(2)}) copy-start(f32[512]{0:T(512)S(1)} %broadcast_multiply_fusion.3) | copy-start | bytes 6148
  31.0 145.1 %copy-start.55 = (f32[512]{0:T(512)}, f32[512]{0:T(512)S(1)}, u32[]{:S(2)}) copy-start(f32[512]{0:T(512)S(1)} %fusion.80) | copy-start | bytes 6148
  31.0 145.0 %copy-start.51 = (f32[768]{0:T(1024)}, f32[768]{0:T(1024)S(1)}, u32[]{:S(2)}) copy-start(f32[768]{0:T(1024)S(1)} %get-tuple-element.122) | copy-start | bytes 9220
  32.2 143.8 %reduce-scatter.7.cloned.1.call-start = ((), (), s32[]{:S(2)}) async-start(), calls=%async_computation.7 | async-start | bytes 3932160 | tf_op jit(solution)/shard_map/reduce_scatter | solution.py:99
  117.0 148.3 %all-gather.5.cloned.1.call-start = ((), (), s32[]{:S(2)}) async-start(), calls=%async_computation.8 | async-start | bytes 3932160 | tf_op jit(solution)/shard_map/all_gather | solution.py:96
  201.6 141.1 %reduce-scatter.9.cloned.1.call-start = ((), (), s32[]{:S(2)}) async-start(), calls=%async_computation.9 | async-start | bytes 3932160 | tf_op jit(solution)/shard_map/reduce_scatter | solution.py:99
  283.7 245.9 %reduce-scatter.11.cloned.1.call-start = ((), (), s32[]{:S(2)}) async-start(), calls=%async_computation.10 | async-start | bytes 3932160 | tf_op jit(solution)/shard_map/reduce_scatter | solution.py:146
  349.8 19.4 %collective-permute-start = (bf16[512,768]{1,0:T(8,128)(2,1)}, bf16[512,768]{1,0:T(8,128)(2,1)}, u32[]{:S(2)}, u32[]{:S(2)}) collective-permute-start(bf16[512,768]{1,0:T(8,128)(2,1)} %add_convert_fusion.7), channel_id=1, source_target_pairs={{0,1},{1,0},{2,3},{3,2},{4,5},{5,4},{6,7},{7,6},{8,9},{9,8},{10,11... | collective-permute-start | bytes 2359304 | tf_op jit(solution)/shard_map/ppermute | solution.py:19
  372.7 70.3 %collective-permute-start.1 = (bf16[1024,768]{1,0:T(8,128)(2,1)}, bf16[1024,768]{1,0:T(8,128)(2,1)}, u32[]{:S(2)}, u32[]{:S(2)}) collective-permute-start(bf16[1024,768]{1,0:T(8,128)(2,1)} %maximum_select_fusion.2), channel_id=1, source_target_pairs={{0,2},{1,3},{2,0},{3,1},{4,6},{5,7},{6,4},{7,5},{8,10},{9,11},{10,... | collective-permute-start | bytes 4718600 | tf_op jit(solution)/shard_map/ppermute | solution.py:19
  375.4 85.4 %copy-start.39 = (bf16[96,8,2,768]{3,1,2,0:T(8,128)(2,1)S(1)}, bf16[96,8,2,768]{3,1,2,0:T(8,128)(2,1)}, u32[]{:S(2)}) copy-start(bf16[96,8,2,768]{3,1,2,0:T(8,128)(2,1)} %copy.112) | copy-start | bytes 7077892
  469.1 275.1 %reduce-scatter.13.cloned.1.call-start = ((), (), s32[]{:S(2)}) async-start(), calls=%async_computation.11 | async-start | bytes 3932160 | tf_op jit(solution)/shard_map/reduce_scatter | solution.py:146
  568.2 91.3 %copy-start.72 = (bf16[2,768,768]{2,1,0:T(8,128)(2,1)S(1)}, bf16[2,768,768]{2,1,0:T(8,128)(2,1)}, u32[]{:S(2)}) copy-start(bf16[2,768,768]{2,1,0:T(8,128)(2,1)} %param.20) | copy-start | bytes 7077892
  569.5 19.2 %collective-permute-start.2 = (bf16[512,768]{1,0:T(8,128)(2,1)S(1)}, bf16[512,768]{1,0:T(8,128)(2,1)S(1)}, u32[]{:S(2)}, u32[]{:S(2)}) collective-permute-start(bf16[512,768]{1,0:T(8,128)(2,1)S(1)} %add_convert_fusion.5), channel_id=1, source_target_pairs={{0,1},{1,0},{2,3},{3,2},{4,5},{5,4},{6,7},{7,6},{8,9},{9,8},{10,11... | collective-permute-start | bytes 2359304 | tf_op jit(solution)/shard_map/ppermute | solution.py:19
  589.4 84.7 %copy-start.41 = (bf16[1024,768]{1,0:T(8,128)(2,1)}, bf16[1024,768]{1,0:T(8,128)(2,1)S(1)}, u32[]{:S(2)}) copy-start(bf16[1024,768]{1,0:T(8,128)(2,1)S(1)} %maximum_select_fusion.3) | copy-start | bytes 4718596
  589.4 70.1 %collective-permute-start.3 = (bf16[1024,768]{1,0:T(8,128)(2,1)S(1)}, bf16[1024,768]{1,0:T(8,128)(2,1)S(1)}, u32[]{:S(2)}, u32[]{:S(2)}) collective-permute-start(bf16[1024,768]{1,0:T(8,128)(2,1)S(1)} %maximum_select_fusion.3), channel_id=1, source_target_pairs={{0,2},{1,3},{2,0},{3,1},{4,6},{5,7},{6,4},{7,5},{8,10},{9,11},{10,... | collective-permute-start | bytes 4718600 | tf_op jit(solution)/shard_map/ppermute | solution.py:19
  683.7 106.8 %reduce-scatter.17.cloned.1.call-start = ((), (), s32[]{:S(2)}) async-start(), calls=%async_computation.13 | async-start | bytes 1327104 | tf_op jit(solution)/shard_map/reduce_scatter | solution.py:245
  691.5 133.7 %reduce-scatter.15.cloned.1.call-start = ((), (), s32[]{:S(2)}) async-start(), calls=%async_computation.12 | async-start | bytes 1327104 | tf_op jit(solution)/shard_map/reduce_scatter | solution.py:245
  717.5 198.0 %all-reduce.14.cloned.1.call-start = ((), (), s32[]{:S(2)}) async-start(), calls=%async_computation.15 | async-start | bytes 9437184
  741.6 488.6 %all-reduce.12.cloned.1.call-start = ((), (), s32[]{:S(2)}) async-start(), calls=%async_computation.14 | async-start | bytes 37748736 | tf_op jit(solution)/shard_map/psum | solution.py:238
  787.7 176.1 %copy-start.20 = (f32[512,768]{1,0:T(8,128)S(1)}, f32[512,768]{1,0:T(8,128)}, u32[]{:S(2)}) copy-start(f32[512,768]{1,0:T(8,128)} %copy-done.18) | copy-start | bytes 4718596
  787.7 176.1 %copy-start.35 = (bf16[12,64,512]{2,1,0:T(8,128)(2,1)S(1)}, bf16[12,64,512]{2,1,0:T(8,128)(2,1)}, u32[]{:S(2)}) copy-start(bf16[12,64,512]{2,1,0:T(8,128)(2,1)} %copy-done.34) | copy-start | bytes 2359300
  787.8 176.1 %copy-start.45 = (bf16[12,64,512]{2,1,0:T(8,128)(2,1)S(1)}, bf16[12,64,512]{2,1,0:T(8,128)(2,1)}, u32[]{:S(2)}) copy-start(bf16[12,64,512]{2,1,0:T(8,128)(2,1)} %copy-done.44) | copy-start | bytes 2359300
  (82 other events, 520.1 us)
Sparse Core Ops, SparseCore 0:
  32.4 66.1 all-gather.2
  117.1 58.8 reduce-scatter.6
  201.7 63.5 all-gather.4
  283.8 58.8 reduce-scatter.8
  469.2 60.3 reduce-scatter.10
  683.8 60.3 reduce-scatter.12
  747.9 36.8 reduce-scatter.16
  788.4 36.7 reduce-scatter.14
  828.5 86.9 all-reduce.13
  923.5 306.5 all-reduce.11
